TPU v7x, 32 devices: a whole 2x2x4 slice. The times are simulated.
32 devices in a mesh: grp: 4 (over z), dom: 8 (over y, x, core).
Axes of the slice: x: 2, y: 2, z: 4, core: 2. Of those that a mesh axis runs over, the one named last changes fastest.
Arguments:
- operator_blocks: float32 [128, 16, 4096], P(('grp', 'dom')), may hold values from -0.75 to 0.75
- operator_cols: int32 [128, 16], P(('grp', 'dom')), may hold values from 0 to 15, as said below
- halo_count: int32 [128], P(('grp', 'dom')), may hold values from 2 to 4, as said below
- prolong_blocks: float32 [128, 8, 4096], P(('grp', 'dom')), may hold values from -0.75 to 0.75
- prolong_cols: int32 [128, 8], P(('grp', 'dom')), may hold values from 0 to 63, as said below
- prolong_slot: int32 [128, 8], P(('grp', 'dom')), may hold values from 0 to 15, as said below
- send_lists: int32 [32, 8], P(('grp', 'dom')), may hold values from 0 to 3
- slot_owner_row: int32 [32, 16], P(('grp', 'dom')), may hold values from 0 to 2, as said below
- coarse_pattern: int32 [64, 16], P(('grp', 'dom')), may hold values from 0 to 63, as said below
Outputs:
- coarse_blocks: float32 [64, 16, 4096], P(('grp', 'dom'))
Inputs may be any that keep to these rules, and one draw needn't show every extreme that they name: `operator_cols`: slots below 12 hold values below 16, the others values below 8. Slots at or beyond a row's live count hold valid values whose blocks do not count. `halo_count`: the first fine row of every device has 4. `prolong_cols`: the 8 values of a row are different. A row on grp index g names coarse rows owned by devices of grp index g only. Slot t of device v stands for owner dom index t // 2 and owner coarse row slot_owner_row[v, t]; prolong_cols[i, j] = ((v // 8) * 8 + s // 2) * 2 + slot_owner_row[v, s] for s = prolong_slot[i, j]; the slots of a row are different and never empty. `slot_owner_row`: the value 2 marks an empty slot; the live values of one device for one owner are different; every device fills all 2 slots of its own dom index and the first slot of every owner, and no other slot. `coarse_pattern`: the 16 values of a row are different.
All inputs are finite; a program needn't handle non-finite values.
Results may differ from a plain program's by a relative error of at most 0.0003.
Values sent between devices are 32-bit elements; how exact they have to be, the bound alone decides.
A program may use at most 128 MiB of HBM per device.

v0:
```python
import functools

import jax
import jax.numpy as jnp
from jax import lax
from jax.experimental import pallas as pl
from jax.experimental.pallas import tpu as pltpu
from jax.sharding import PartitionSpec as P

BS = 64
KG = 12
KH = 4
LANES = 128


def any_spec():
    return pl.BlockSpec(memory_space=pl.ANY)


def vmem_spec():
    return pl.BlockSpec(memory_space=pltpu.VMEM)


def smem_spec():
    return pl.BlockSpec(memory_space=pltpu.SMEM)


def prepare_rows(
    n_dom, rows, hs, kp, kc, cap,
    picked, owner, prolong_raw, prolong_cols, pattern,
    panels, outgoing, prolong, dom_meta, grp_meta,
):
    owned = pattern.shape[0]
    for i in range(rows):
        raw = prolong_raw[i]
        for a in range(BS):
            prolong[i, :, a, :] = raw[:, a * BS:(a + 1) * BS]
        for q in range(0, kp, 2):
            panels[i, :, q * BS:(q + 2) * BS] = jnp.concatenate([prolong[i, q], prolong[i, q + 1]], axis=1)
    grp_meta[...] = jnp.zeros(grp_meta.shape, jnp.int32)
    dom_meta[...] = jnp.zeros(dom_meta.shape, jnp.int32)
    for i in range(rows):
        grp_meta[:, i * kp:(i + 1) * kp] = prolong_cols[i:i + 1, :]
    row_at = hs * kp + owned * kc

    def for_dom(d, carry):
        for h in range(hs):
            row = picked[0, d * hs + h]
            outgoing[d * hs + h] = panels[row]
            dom_meta[d, :, h * kp:(h + 1) * kp] = prolong_cols[pl.ds(row, 1), :]
        for r in range(owned):
            at = hs * kp + r * kc
            dom_meta[d, :, at:at + kc] = pattern[r:r + 1, :]
        dom_meta[d, :, row_at:row_at + 1] = jnp.full((1, 1), owner[0, d * cap], jnp.int32)
        return carry

    lax.fori_loop(0, n_dom, for_dom, 0)


def gather_kernel(
    n_grp, n_dom, rows, hs, kp, kc, cap,
    halo, picked, owner, prolong_raw, prolong_cols, pattern, operator_in,
    table, meta, stacked_out, prolong_out,
    operator, stacked, prolong, bulk_sem,
    panels, outgoing, dom_meta, grp_meta, blocks, own_sem, line_send, line_recv, dom_send, dom_recv, meta_send, meta_recv,
):
    g = lax.axis_index("grp")
    me = lax.axis_index("dom")
    far_base = n_grp * rows
    barrier = pltpu.get_barrier_semaphore()
    for k in range(1, n_grp):
        pl.semaphore_signal(barrier, inc=1, device_id={"grp": lax.rem(g + k, n_grp)})
    for k in range(1, n_dom):
        pl.semaphore_signal(barrier, inc=1, device_id={"dom": lax.rem(me + k, n_dom)})
    operator_copy = pltpu.make_async_copy(operator_in, operator, bulk_sem.at[0])
    operator_copy.start()
    prepare_rows(
        n_dom, rows, hs, kp, kc, cap,
        picked, owner, prolong_raw, prolong_cols, pattern,
        panels, outgoing, prolong, dom_meta, grp_meta,
    )
    pl.semaphore_wait(barrier, n_grp + n_dom - 2)

    def line_copy(direction, step, r, src, origin):
        target = g + 1 if direction == 0 else g - 1
        return pltpu.make_async_remote_copy(
            src_ref=src,
            dst_ref=table.at[origin * rows + r],
            send_sem=line_send.at[direction, step, r],
            recv_sem=line_recv.at[direction, step, r],
            device_id={"grp": target},
        )

    can_send = (g < n_grp - 1, g > 0)
    for r in range(rows):
        for direction in range(2):
            @pl.when(can_send[direction])
            def _():
                line_copy(direction, 0, r, panels.at[r], g).start()

    def meta_copy(k, over_dom):
        if over_dom:
            target = lax.rem(me + k, n_dom)
            return pltpu.make_async_remote_copy(
                src_ref=dom_meta.at[target], dst_ref=meta.at[n_grp + me],
                send_sem=meta_send.at[n_grp + k], recv_sem=meta_recv.at[n_grp + k],
                device_id={"dom": target},
            )
        return pltpu.make_async_remote_copy(
            src_ref=grp_meta, dst_ref=meta.at[g],
            send_sem=meta_send.at[k], recv_sem=meta_recv.at[k],
            device_id={"grp": lax.rem(g + k, n_grp)},
        )

    def dom_copy(k):
        target = lax.rem(me + k, n_dom)
        return pltpu.make_async_remote_copy(
            src_ref=outgoing.at[pl.ds(target * hs, hs)],
            dst_ref=table.at[pl.ds(far_base + me * hs, hs)],
            send_sem=dom_send.at[k], recv_sem=dom_recv.at[k],
            device_id={"dom": target},
        )

    for k in range(1, n_grp):
        meta_copy(k, False).start()
    for k in range(1, n_dom):
        dom_copy(k).start()
        meta_copy(k, True).start()
    own = (
        pltpu.make_async_copy(panels, table.at[pl.ds(g * rows, rows)], own_sem.at[0]),
        pltpu.make_async_copy(outgoing.at[pl.ds(me * hs, hs)], table.at[pl.ds(far_base + me * hs, hs)], own_sem.at[1]),
        pltpu.make_async_copy(grp_meta, meta.at[g], own_sem.at[2]),
        pltpu.make_async_copy(dom_meta.at[me], meta.at[n_grp + me], own_sem.at[3]),
    )
    for copy in own:
        copy.start()

    def relay_row(i, carry):
        row = operator[i]
        for a in range(BS):
            blocks[i, :, a, :] = row[:, a * BS:(a + 1) * BS]
        return carry

    def split_row(i, carry):
        for m in range(blocks.shape[1]):
            block = blocks[i, m]
            if m >= KG:
                block = jnp.where(m - KG < halo[i], block, 0.0)
            high = block.astype(jnp.bfloat16).astype(jnp.float32)
            stacked[i, m] = jnp.concatenate([high, high, block - high], axis=1).astype(jnp.bfloat16)
        return carry

    prolong_copy = pltpu.make_async_copy(prolong, prolong_out, bulk_sem.at[1])
    stacked_copy = pltpu.make_async_copy(stacked, stacked_out, bulk_sem.at[2])
    prolong_copy.start()
    operator_copy.wait()
    lax.fori_loop(0, rows, relay_row, 0)
    lax.fori_loop(0, rows, split_row, 0)
    stacked_copy.start()

    def origin_of(direction, step):
        return g - 1 - step if direction == 0 else g + 1 + step

    for step in range(n_grp - 1):
        for r in range(rows):
            for direction in range(2):
                origin = origin_of(direction, step)
                exists = (origin >= 0) & (origin < n_grp)

                @pl.when(exists)
                def _():
                    src = table.at[origin * rows + r]
                    line_copy(direction, step, r, src, origin).wait_recv()

                if step < n_grp - 2:
                    @pl.when(exists & can_send[direction])
                    def _():
                        src = table.at[origin * rows + r]
                        line_copy(direction, step + 1, r, src, origin).start()

    prolong_copy.wait()
    stacked_copy.wait()
    for copy in own:
        copy.wait()
    for k in range(1, n_grp):
        meta_copy(k, False).wait()
    for k in range(1, n_dom):
        dom_copy(k).wait()
        meta_copy(k, True).wait()
    for step in range(n_grp - 1):
        for r in range(rows):
            for direction in range(2):
                origin = g - step if direction == 0 else g + step
                exists = (origin >= 0) & (origin < n_grp)

                @pl.when(exists & can_send[direction])
                def _():
                    line_copy(direction, step, r, panels.at[r], origin).wait_send()


def split_pair(x):
    high = x.astype(jnp.bfloat16)
    low = (x - high.astype(jnp.float32)).astype(jnp.bfloat16)
    return high, low


def product_kernel(
    n_grp, n_dom, rows, hs, ka, kp,
    cols, meta,
    operator_in, table_in,
    out,
    operator, table, split_table, total, load_sem,
):
    k = pl.program_id(0)
    panel_count = table.shape[0]
    near_count = n_grp * rows
    lane = lax.broadcasted_iota(jnp.int32, (BS, LANES), 1) < BS

    @pl.when(k == 0)
    def _():
        table_copy = pltpu.make_async_copy(table_in, table, load_sem.at[0])
        operator_copy = pltpu.make_async_copy(operator_in, operator, load_sem.at[1])
        table_copy.start()
        operator_copy.start()

        def clear(e, carry):
            total[e] = jnp.zeros(total.shape[1:], jnp.float32)
            return carry

        lax.fori_loop(0, total.shape[0], clear, 0)

        def split(p, carry):
            high, low = split_pair(table[p])
            split_table[p, 0:BS] = high
            split_table[p, BS:2 * BS] = low
            split_table[p, 2 * BS:3 * BS] = high
            return carry

        table_copy.wait()
        lax.fori_loop(0, panel_count, split, 0)
        operator_copy.wait()

        def pairs(m, carry):
            near = m < KG
            products = []
            places = []
            for i in range(rows):
                col = cols[i, m]
                panel = jnp.where(near, col, near_count + col)
                meta_row = jnp.where(near, col // rows, n_grp + col // hs)
                meta_lane = jnp.where(near, (col % rows) * kp, (col % hs) * kp)
                products.append(
                    jnp.dot(operator[i, m], split_table[panel], preferred_element_type=jnp.float32)
                )
                places.append((meta_row, meta_lane))
            for i in range(rows):
                for start in range(0, kp, 4):
                    updates = []
                    for q in range(start, min(start + 4, kp), 2):
                        piece = products[i][:, q * BS:(q + 2) * BS]
                        turned = pltpu.roll(piece, BS, 1)
                        first = meta[places[i][0], 0, places[i][1] + q]
                        second = meta[places[i][0], 0, places[i][1] + q + 1]
                        updates.append((first, total[first, i] + jnp.where(lane, piece, turned)))
                        updates.append((second, total[second, i] + jnp.where(lane, turned, piece)))
                    for place, value in updates:
                        total[place, i] = value
            return carry

        lax.fori_loop(0, ka, pairs, 0)

    chunk = out.shape[0]
    half = lax.broadcasted_iota(jnp.int32, (rows * BS, LANES), 1) < BS

    def fold(t, carry):
        value = total[k * chunk + t].reshape(rows * BS, LANES)
        high = value.astype(jnp.bfloat16).astype(jnp.float32)
        out[t] = jnp.where(half, high, value - high).astype(jnp.bfloat16)
        return carry

    lax.fori_loop(0, chunk, fold, 0, unroll=4)


def exchange_kernel(
    n_grp, n_dom, rows, hs, kp, kc, cap, row_at,
    slots, owner, meta, packed_in, prolong_in,
    out,
    packed, prolong, load_sem, partial, arrived, summed, send_sem, recv_sem,
):
    me = lax.axis_index("dom")
    loads = (
        pltpu.make_async_copy(packed_in, packed, load_sem.at[0]),
        pltpu.make_async_copy(prolong_in, prolong, load_sem.at[1]),
    )
    for load in loads:
        load.start()
    barrier = pltpu.get_barrier_semaphore()
    for k in range(1, n_dom):
        pl.semaphore_signal(barrier, inc=1, device_id={"dom": lax.rem(me + k, n_dom)})
    pl.semaphore_wait(barrier, n_dom - 1)
    for load in loads:
        load.wait()
    lane = lax.broadcasted_iota(jnp.int32, (BS, LANES), 1) < BS

    def slot_rows(owner_dom, slot, at):
        owner_row = owner[0, slot]
        pattern_at = hs * kp + owner_row * kc
        left = []
        for i in range(rows):
            place = jnp.int32(kp)
            for j in range(kp):
                place = jnp.where(slots[i, j] == slot, j, place)
            block = prolong[i, jnp.minimum(place, kp - 1)]
            left.append(jnp.where(place < kp, block, 0.0).T)
        left_high, left_low = split_pair(jnp.concatenate(left, axis=1))
        both = jnp.concatenate([left_high, left_low], axis=0)
        for c in range(0, kc, 2):
            right = jnp.concatenate(
                [packed[meta[n_grp + owner_dom, 0, pattern_at + c + h]] for h in range(2)], axis=1
            )
            stacked = jnp.dot(both, right, preferred_element_type=jnp.float32)
            both_sum = stacked[:BS] + stacked[BS:]
            folded = []
            for h in range(2):
                piece = both_sum[:, h * LANES:(h + 1) * LANES]
                folded.append(piece + pltpu.roll(piece, BS, 1))
            partial[at, :, c * BS:(c + 2) * BS] = jnp.where(lane, folded[0], folded[1])

    assert n_dom & (n_dom - 1) == 0

    def partner(k):
        other = 0
        bit = 1
        while bit < n_dom:
            other += lax.rem(me // bit + k // bit, 2) * bit
            bit *= 2
        return other

    def copy_of(k):
        target = partner(k)
        return pltpu.make_async_remote_copy(
            src_ref=partial.at[k], dst_ref=arrived.at[k - 1],
            send_sem=send_sem.at[k - 1], recv_sem=recv_sem.at[k - 1],
            device_id={"dom": target},
        )

    def far_slot(step, carry):
        k = n_dom - step
        target = partner(k)
        slot_rows(target, target * cap, k)

        @pl.when(step > 1)
        def _():
            copy_of(k + 1).start()

        return carry

    lax.fori_loop(1, n_dom, far_slot, 0)
    slot_rows(me, me * cap, 0)
    copy_of(1).start()
    owned = out.shape[0]
    for r in range(owned):
        summed[r] = partial[0] * (owner[0, me * cap] == r).astype(jnp.float32)
    for t in range(1, cap):
        slot_rows(me, me * cap + t, n_dom + t - 1)
        for r in range(owned):
            summed[r] += partial[n_dom + t - 1] * (owner[0, me * cap + t] == r).astype(jnp.float32)
    for k in range(n_dom - 1, 0, -1):
        copy_of(k).wait_recv()
        source = partner(k)
        row = meta[n_grp + source, 0, row_at]
        for r in range(owned):
            summed[r] += arrived[k - 1] * (row == r).astype(jnp.float32)
    for r in range(owned):
        for c in range(kc):
            out[r, c] = summed[r, :, c * BS:(c + 1) * BS]
    for k in range(1, n_dom):
        copy_of(k).wait_send()


def per_device(
    operator_blocks, operator_cols, halo_count, prolong_blocks, prolong_cols,
    prolong_slot, send_lists, slot_owner_row, coarse_pattern,
):
    n_grp = lax.axis_size("grp")
    n_dom = lax.axis_size("dom")
    rows, ka = operator_cols.shape
    kp = prolong_cols.shape[1]
    owned, kc = coarse_pattern.shape
    hs = send_lists.shape[1] // n_dom
    cap = slot_owner_row.shape[1] // n_dom
    total_ids = owned * n_grp * n_dom
    used = n_dom + cap - 1
    panel_count = n_grp * rows + n_dom * hs
    row_at = hs * kp + owned * kc
    f32 = lambda *shape: jax.ShapeDtypeStruct(shape, jnp.float32)
    i32 = lambda *shape: jax.ShapeDtypeStruct(shape, jnp.int32)

    sem = pltpu.SemaphoreType.DMA
    table, meta, stacked, prolong = pl.pallas_call(
        functools.partial(gather_kernel, n_grp, n_dom, rows, hs, kp, kc, cap),
        out_shape=(
            f32(panel_count, BS, kp * BS), i32(n_grp + n_dom, 1, LANES),
            jax.ShapeDtypeStruct((rows, ka, BS, 3 * BS), jnp.bfloat16), f32(rows, kp, BS, BS),
        ),
        in_specs=[smem_spec()] * 3 + [vmem_spec()] * 3 + [any_spec()],
        out_specs=(any_spec(),) * 4,
        scratch_shapes=[
            pltpu.VMEM((rows, ka, BS * BS), jnp.float32),
            pltpu.VMEM((rows, ka, BS, 3 * BS), jnp.bfloat16),
            pltpu.VMEM((rows, kp, BS, BS), jnp.float32),
            sem((3,)),
            pltpu.VMEM((rows, BS, kp * BS), jnp.float32),
            pltpu.VMEM((n_dom * hs, BS, kp * BS), jnp.float32),
            pltpu.VMEM((n_dom, 1, LANES), jnp.int32),
            pltpu.VMEM((1, LANES), jnp.int32),
            pltpu.VMEM((rows, ka, BS, BS), jnp.float32),
            sem((4,)), sem((2, n_grp - 1, rows)), sem((2, n_grp - 1, rows)),
            sem((n_dom,)), sem((n_dom,)), sem((n_grp + n_dom,)), sem((n_grp + n_dom,)),
        ],
        compiler_params=pltpu.CompilerParams(collective_id=0, has_side_effects=True),
        name="gather_rows",
    )(
        halo_count, send_lists, slot_owner_row, prolong_blocks, prolong_cols, coarse_pattern, operator_blocks
    )

    chunk = 8
    packed = pl.pallas_call(
        functools.partial(product_kernel, n_grp, n_dom, rows, hs, ka, kp),
        grid=(total_ids // chunk,),
        out_shape=jax.ShapeDtypeStruct((total_ids, rows * BS, LANES), jnp.bfloat16),
        in_specs=[smem_spec()] * 2 + [any_spec()] * 2,
        out_specs=pl.BlockSpec((chunk, rows * BS, LANES), lambda k: (k, 0, 0)),
        scratch_shapes=[
            pltpu.VMEM((rows, ka, BS, 3 * BS), jnp.bfloat16),
            pltpu.VMEM((panel_count, BS, kp * BS), jnp.float32),
            pltpu.VMEM((panel_count, 3 * BS, kp * BS), jnp.bfloat16),
            pltpu.VMEM((total_ids, rows, BS, LANES), jnp.float32),
            sem((2,)),
        ],
        compiler_params=pltpu.CompilerParams(vmem_limit_bytes=63000 * 1024),
        name="block_products",
    )(operator_cols, meta, stacked, table)

    summed = pl.pallas_call(
        functools.partial(exchange_kernel, n_grp, n_dom, rows, hs, kp, kc, cap, row_at),
        out_shape=f32(owned, kc, BS, BS),
        in_specs=[smem_spec()] * 3 + [any_spec()] * 2,
        out_specs=vmem_spec(),
        scratch_shapes=[
            pltpu.VMEM((total_ids, rows * BS, LANES), jnp.bfloat16),
            pltpu.VMEM((rows, kp, BS, BS), jnp.float32),
            sem((2,)),
            pltpu.VMEM((used, BS, kc * BS), jnp.float32),
            pltpu.VMEM((n_dom - 1, BS, kc * BS), jnp.float32),
            pltpu.VMEM((owned, BS, kc * BS), jnp.float32),
            sem((n_dom - 1,)), sem((n_dom - 1,)),
        ],
        compiler_params=pltpu.CompilerParams(
            collective_id=1, has_side_effects=True, vmem_limit_bytes=63000 * 1024
        ),
        name="sum_rows",
    )(prolong_slot, slot_owner_row, meta, packed, prolong)
    return summed.reshape(owned, kc, BS * BS)


def solution(mesh):
    blocks = P(("grp", "dom"), None, None)
    lists = P(("grp", "dom"), None)
    return jax.shard_map(
        per_device,
        mesh=mesh,
        in_specs=(blocks, lists, P(("grp", "dom")), blocks, lists, lists, lists, lists, lists),
        out_specs=blocks,
        check_vma=False,
    )
```

profile of v0, /device:TPU:0, one launch (start us, length us, event | category | flops | bytes accessed | tf_op | source)
XLA Modules:
  0.0 89.5 jit_solution(16708033460018394470)
XLA Ops:
  0.0 42.4 %gather_rows.1 = (f32[24,64,512]{2,1,0:T(8,128)}, s32[12,1,128]{2,1,0:T(1,128)}, bf16[4,16,64,192]{3,2,1,0:T(8,128)(2,1)}, f32[4,8,64,64]{3,2,1,0:T(8,128)}) custom-call(s32[4]{0:T(128)} %halo.1, s32[1,8]{1,0:T(1,128)} %picked.1, s32[1,16]{1,0:T(1,128)} %owner.3, f32[4,8,4096]{2,1,0:T(8,128)} %prolong_raw.1, s32[4,8]{1,0:T(4,128)} %prolong_cols.1, ...), custom_call_target="tpu_custom_call" | custom-call | tf_op jit(solution)/shard_map/gather_rows/pallas_call | solution.py:400
  42.4 14.5 %block_products.1.packed_in = bf16[64,256,128]{2,1,0:T(8,128)(2,1)} custom-call(s32[4,16]{1,0:T(4,128)} %cols.1, s32[12,1,128]{2,1,0:T(1,128)} %get-tuple-element.9.meta, bf16[4,16,64,192]{3,2,1,0:T(8,128)(2,1)} %get-tuple-element.10.operator_in, f32[24,64,512]{2,1,0:T(8,128)} %get-tuple-element.11.table_in), custom_call_target="tpu_custom_call" | custom-call | tf_op jit(solution)/shard_map/block_products/pallas_call | solution.py:428
  56.8 30.3 %sum_rows.1 = f32[2,16,64,64]{3,2,1,0:T(8,128)} custom-call(s32[4,8]{1,0:T(4,128)} %slots.1, s32[1,16]{1,0:T(1,128)} %owner.3, s32[12,1,128]{2,1,0:T(1,128)} %get-tuple-element.9.meta, bf16[64,256,128]{2,1,0:T(8,128)(2,1)} %block_products.1.packed_in, f32[4,8,64,64]{3,2,1,0:T(8,128)} %get-tuple-element.12.prolong_in), custom_call_target="tpu_custom_call" | custom-call | tf_op jit(solution)/shard_map/sum_rows/pallas_call | solution.py:445
  87.1 2.4 %reshape.3 = f32[2,16,4096]{2,1,0:T(8,128)} reshape(f32[2,16,64,64]{3,2,1,0:T(8,128)} %sum_rows.1) | data formatting | bytes 1048576 | tf_op jit(solution)/shard_map/reshape | solution.py:464
where the time goes:
time: 89.8 us; the launch traced here: 89.5 us
  Pallas kernels  87.1 us (97%)
  local copies, waits for them, and re-layouts  2.37 us (3%)
    pallas_call x1, Pallas kernels, per_device(): pl.pallas_call(functools.partial(gather_kernel, n_grp, n_dom, rows, hs, k...  42.4 us
    pallas_call x1, Pallas kernels, per_device(): pl.pallas_call(functools.partial(exchange_kernel, n_grp, n_dom, rows, hs,...  30.3 us
    pallas_call x1, Pallas kernels, per_device(): pl.pallas_call(functools.partial(product_kernel, n_grp, n_dom, rows, hs,...  14.5 us
    reshape x1, local copies, waits for them, and re-layouts, per_device(): return summed.reshape(owned, kc, BS * BS)  2.37 us

commit v1 on v0

v1 whole, which is shorter than its diff:
```python
import functools

import jax
import jax.numpy as jnp
from jax import lax
from jax.experimental import pallas as pl
from jax.experimental.pallas import tpu as pltpu
from jax.sharding import PartitionSpec as P

BS = 64
KG = 12
LANES = 128
SUB = 8


def any_spec():
    return pl.BlockSpec(memory_space=pl.ANY)


def vmem_spec():
    return pl.BlockSpec(memory_space=pltpu.VMEM)


def smem_spec():
    return pl.BlockSpec(memory_space=pltpu.SMEM)


def fused_kernel(
    n_grp, n_dom, rows, hs, ka, kp, kc, cap, owned, stages,
    cols, halo, slots, picked, owner, prolong_cols, pattern, prolong_in, operator_in,
    out,
    own_raw, operator, table, outgoing, grp_out, grp_in, dom_base, dom_out, dom_in, plan_v, plan_s,
    blocks, dense, own_dup, stage, panels, left, ap, partial, arrived, summed,
    load_sem, line_send, line_recv, halo_send, halo_recv,
    gmeta_send, gmeta_recv, dmeta_send, dmeta_recv, plan_sem, part_send, part_recv,
):
    g = lax.axis_index("grp")
    me = lax.axis_index("dom")
    near_count = n_grp * rows
    plane_ids = owned * n_dom
    halo_count_rows = n_dom * hs
    groups = n_grp + halo_count_rows // rows
    zero_at = (rows + halo_count_rows) * kp
    row_at = hs + owned
    sort_at = n_grp + n_dom
    rank_at = sort_at + n_dom
    width = rows * BS
    tiles = BS // 2
    low = lax.broadcasted_iota(jnp.int32, (1, LANES), 1) < BS
    lane = lax.broadcasted_iota(jnp.int32, (SUB, LANES), 1)
    sub = lax.broadcasted_iota(jnp.int32, (SUB, LANES), 0)

    barrier = pltpu.get_barrier_semaphore()
    for k in range(1, n_grp):
        pl.semaphore_signal(barrier, inc=1, device_id={"grp": lax.rem(g + k, n_grp)})
    for k in range(1, n_dom):
        pl.semaphore_signal(barrier, inc=1, device_id={"dom": lax.rem(me + k, n_dom)})
    own_load = pltpu.make_async_copy(prolong_in, own_raw, load_sem.at[0])
    operator_load = pltpu.make_async_copy(operator_in, operator, load_sem.at[1])
    own_load.start()
    operator_load.start()

    def partner(k):
        other = 0
        bit = 1
        while bit < n_dom:
            other += lax.rem(me // bit + k // bit, 2) * bit
            bit *= 2
        return other

    grp_out[...] = jnp.zeros(grp_out.shape, jnp.int32)
    grp_out[0:rows, 0:kp] = prolong_cols[...]
    dom_base[...] = jnp.zeros(dom_base.shape, jnp.int32)
    for r in range(owned):
        for j in range(0, LANES, kc):
            dom_base[hs + r:hs + r + 1, j:j + kc] = pattern[r:r + 1, :]

    def for_dom(d, carry):
        dom_out[d] = dom_base[...]
        for h in range(hs):
            dom_out[d, h:h + 1, 0:kp] = prolong_cols[pl.ds(picked[0, d * hs + h], 1), :]
        dom_out[d, row_at:row_at + 1, :] = jnp.full((1, LANES), owner[0, d * cap], jnp.int32)
        return carry

    lax.fori_loop(0, n_dom, for_dom, 0)
    grp_in[g] = grp_out[...]
    dom_in[me] = dom_out[me]
    pl.semaphore_wait(barrier, n_grp + n_dom - 2)

    def line_copy(direction, step, r, src, origin):
        return pltpu.make_async_remote_copy(
            src_ref=src, dst_ref=table.at[origin * rows + r],
            send_sem=line_send.at[direction, step, r], recv_sem=line_recv.at[direction, step, r],
            device_id={"grp": g + 1 if direction == 0 else g - 1},
        )

    def grp_meta(k):
        return pltpu.make_async_remote_copy(
            src_ref=grp_out, dst_ref=grp_in.at[g], send_sem=gmeta_send.at[k], recv_sem=gmeta_recv.at[k],
            device_id={"grp": lax.rem(g + k, n_grp)},
        )

    def dom_meta(k):
        target = partner(k)
        return pltpu.make_async_remote_copy(
            src_ref=dom_out.at[target], dst_ref=dom_in.at[me], send_sem=dmeta_send.at[k], recv_sem=dmeta_recv.at[k],
            device_id={"dom": target},
        )

    def halo_copy(k):
        target = partner(k)
        return pltpu.make_async_remote_copy(
            src_ref=outgoing.at[pl.ds(target * hs, hs)], dst_ref=table.at[pl.ds(near_count + me * hs, hs)],
            send_sem=halo_send.at[k], recv_sem=halo_recv.at[k],
            device_id={"dom": target},
        )

    for k in range(1, n_grp):
        grp_meta(k).start()

    def start_dom_meta(k, carry):
        dom_meta(k).start()
        return carry

    lax.fori_loop(1, n_dom, start_dom_meta, 0)
    can_send = (g < n_grp - 1, g > 0)
    for r in range(rows):
        for direction in range(2):
            @pl.when(can_send[direction])
            def _():
                line_copy(direction, 0, r, prolong_in.at[r], g).start()

    own_load.wait()

    def pick(n, carry):
        outgoing[n] = own_raw[picked[0, n]]
        return carry

    lax.fori_loop(0, halo_count_rows, pick, 0)

    def duplicate(x, write, at):
        turned = pltpu.roll(x, BS, 1)
        write(at, jnp.where(low, x, turned))
        write(at + 1, jnp.where(low, turned, x))

    def own_row(i, carry):
        def write(a, value):
            own_dup[pl.ds(i * kp, kp), a, :] = value

        for t in range(tiles):
            duplicate(own_raw[i, :, t * LANES:(t + 1) * LANES], write, 2 * t)
        return carry

    lax.fori_loop(0, rows, own_row, 0)

    def start_halo(k, carry):
        halo_copy(k).start()
        return carry

    lax.fori_loop(1, n_dom, start_halo, 0)
    own_dup[rows * kp] = jnp.zeros((BS, LANES), jnp.float32)
    panels[zero_at] = jnp.zeros((2 * BS, LANES), jnp.bfloat16)

    def split(value):
        high = value.astype(jnp.bfloat16)
        return high, (value - high.astype(jnp.float32)).astype(jnp.bfloat16)

    def keep(at, value):
        high, rest = split(value)
        panels[at, 0:BS] = high
        panels[at, BS:2 * BS] = rest

    def convert(panel, place):
        def write(a, value):
            stage[:, a, :] = value

        for t in range(tiles):
            duplicate(table[panel, :, t * LANES:(t + 1) * LANES], write, 2 * t)
        for q in range(kp):
            keep(place * kp + q, stage[q])

    operator_load.wait()

    def relay(n, carry):
        i = n // (ka // SUB)
        m = lax.rem(n, ka // SUB) * SUB

        def write(a, value):
            blocks[i, pl.ds(m, SUB), a, :] = value

        for t in range(tiles):
            duplicate(operator[i, pl.ds(m, SUB), t * LANES:(t + 1) * LANES], write, 2 * t)
        return carry

    lax.fori_loop(0, rows * (ka // SUB), relay, 0)

    def densify(i, group, slots_used, column_of):
        for pair in range(0, rows, 2):
            first = group * rows + pair
            wanted = jnp.where(low, first, first + 1)
            total = jnp.zeros((BS, LANES), jnp.float32)
            for m in slots_used:
                total += jnp.where(wanted == column_of(i, m), blocks[i, m], 0.0)
            high, rest = split(total)
            here = pl.ds(i * BS, BS)
            dense[group, here, pair * BS:(pair + 2) * BS] = high
            dense[group, here, width + pair * BS:width + (pair + 2) * BS] = rest

    def near_dense(n, carry):
        densify(n // n_grp, lax.rem(n, n_grp), range(KG), lambda i, m: cols[i, m])
        return carry

    def far_column(i, m):
        return jnp.where(m - KG < halo[i], near_count + cols[i, m], -1)

    far_groups = groups - n_grp

    def far_dense(n, carry):
        densify(n // far_groups, n_grp + lax.rem(n, far_groups), range(KG, ka), far_column)
        return carry

    lax.fori_loop(0, rows * n_grp, near_dense, 0)
    lax.fori_loop(0, rows * far_groups, far_dense, 0)

    for k in range(1, n_grp):
        grp_meta(k).wait()

    def wait_dom_meta(k, carry):
        dom_meta(k).wait()
        return carry

    lax.fori_loop(1, n_dom, wait_dom_meta, 0)

    def places(values, first_id, first_place):
        found = jnp.full((SUB, LANES), zero_at, jnp.int32)
        for q in range(kp):
            found = jnp.where(values[:, q:q + 1] == first_id + lane, (first_place + sub) * kp + q, found)
        return found

    for origin in range(n_grp):
        side = (origin > g).astype(jnp.int32)
        plan_v[origin] = places(grp_in[origin], origin * plane_ids, side * rows)

    slot_of_lane = lax.rem(lane, kc)

    def dom_tables(d, carry):
        values = dom_in[d]
        plan_v[n_grp + d] = places(values, g * plane_ids, rows + d * hs)
        plane = jnp.zeros((SUB, LANES), jnp.int32)
        for n in range(1, n_grp):
            plane += (values >= n * plane_ids).astype(jnp.int32)
        order = jnp.abs(plane - g) * kc + slot_of_lane
        rank = jnp.zeros((SUB, LANES), jnp.int32)
        for s in range(1, kc):
            rank += (pltpu.roll(order, s, 1) < order).astype(jnp.int32)
        ordered = values
        for s in range(kc):
            ordered = jnp.where(pltpu.roll(rank, s, 1) == slot_of_lane, pltpu.roll(values, s, 1), ordered)
        plan_v[sort_at + d] = ordered
        plan_v[rank_at + d] = rank
        return carry

    lax.fori_loop(0, n_dom, dom_tables, 0)
    plan_copy = pltpu.make_async_copy(plan_v, plan_s, plan_sem.at[0])
    plan_copy.start()

    def transposed(slot, at):
        for pair in range(0, rows, 2):
            both = []
            for i in range(pair, pair + 2):
                place = jnp.int32(rows * kp)
                for j in range(kp):
                    place = jnp.where(slots[i, j] == slot, i * kp + j, place)
                both.append(own_dup[place])
            turned = jnp.concatenate(both, axis=0).T
            high = turned.astype(jnp.bfloat16).astype(jnp.float32)
            upper = lax.broadcasted_iota(jnp.int32, (LANES, LANES), 0) < BS
            left[at, :, pair * BS:(pair + 2) * BS] = jnp.where(upper, high, turned - high).astype(jnp.bfloat16)

    def far_left(k, carry):
        transposed(partner(k) * cap, k)
        return carry

    lax.fori_loop(1, n_dom, far_left, 0)
    for t in range(cap):
        transposed(me * cap + t, 0 if t == 0 else n_dom + t - 1)

    def own_panels(n, carry):
        keep(n, own_dup[n])
        return carry

    lax.fori_loop(0, rows * kp, own_panels, 0)
    plan_copy.wait()

    def multiply(plane, parts):
        def four(n, carry):
            e = n * 4
            total = None
            for group, index_of in parts:
                halves = []
                for pair in range(2):
                    blocks_here = [
                        jnp.where(low, panels[index_of(r, e + 2 * pair)], panels[index_of(r, e + 2 * pair + 1)])
                        for r in range(rows)
                    ]
                    high = [b[0:BS] for b in blocks_here]
                    rest = [b[BS:2 * BS] for b in blocks_here]
                    halves.append(jnp.concatenate(high + rest + high, axis=0))
                right = jnp.concatenate(halves, axis=1)
                split_dense = dense[group]
                lhs = jnp.concatenate([split_dense[:, 0:width], split_dense], axis=1)
                product = jnp.dot(lhs, right, preferred_element_type=jnp.float32)
                total = product if total is None else total + product
            for pair in range(2):
                value = total[:, pair * LANES:(pair + 1) * LANES]
                high = value.astype(jnp.bfloat16).astype(jnp.float32)
                rest = value - high
                turned = pltpu.roll(jnp.where(low, rest, high), BS, 1)
                at = plane * plane_ids + e + 2 * pair
                ap[at] = jnp.where(low, high, turned).astype(jnp.bfloat16)
                ap[at + 1] = jnp.where(low, turned, rest).astype(jnp.bfloat16)
            return carry

        lax.fori_loop(0, plane_ids // 4, four, 0)

    def near_index(origin):
        return lambda r, e: plan_s[origin, r, e]

    def far_index(group):
        def index_of(r, e):
            n = group * rows + r
            return plan_s[n_grp + n // hs, n % hs, e]
        return index_of

    def part_copy(s, k):
        first, last = stages[s][1:]
        here = pl.ds(first * BS, (last - first) * BS)
        return pltpu.make_async_remote_copy(
            src_ref=partial.at[k, :, here], dst_ref=arrived.at[k - 1, :, here],
            send_sem=part_send.at[s, k - 1], recv_sem=part_recv.at[s, k - 1],
            device_id={"dom": partner(k)},
        )

    def slot_rows(s, owner_dom, slot, at):
        first, last = stages[s][1:]
        line = hs + owner[0, slot]
        for c in range(first, last, 2):
            right = jnp.concatenate([ap[plan_s[sort_at + owner_dom, line, c + h]] for h in range(2)], axis=1)
            product = jnp.dot(left[at], right, preferred_element_type=jnp.float32)
            both = product[:BS] + product[BS:]
            one, two = both[:, :LANES], both[:, LANES:]
            partial[at, :, c * BS:(c + 2) * BS] = jnp.where(low, one, two) + pltpu.roll(jnp.where(low, two, one), BS, 1)

    def exchange(s):
        first, last = stages[s][1:]
        here = slice(first * BS, last * BS)

        def far_slot(step, carry):
            k = n_dom - step
            target = partner(k)
            slot_rows(s, target, target * cap, k)

            @pl.when(step > 1)
            def _():
                part_copy(s, k + 1).start()

            return carry

        lax.fori_loop(1, n_dom, far_slot, 0)
        slot_rows(s, me, me * cap, 0)
        part_copy(s, 1).start()
        for t in range(1, cap):
            slot_rows(s, me, me * cap + t, n_dom + t - 1)
        for r in range(owned):
            total = partial[0, :, here] * (owner[0, me * cap] == r).astype(jnp.float32)
            for t in range(1, cap):
                total += partial[n_dom + t - 1, :, here] * (owner[0, me * cap + t] == r).astype(jnp.float32)
            summed[r, :, here] = total

    def collect(s):
        first, last = stages[s][1:]

        def one(step, carry):
            k = n_dom - step
            part_copy(s, k).wait_recv()
            row = dom_in[partner(k), row_at:row_at + 1, :]
            for c in range(first, last, 2):
                here = slice(c * BS, (c + 2) * BS)
                value = arrived[k - 1, :, here]
                for r in range(owned):
                    summed[r, :, here] += jnp.where(row == r, value, 0.0)
            return carry

        lax.fori_loop(1, n_dom, one, 0)

    def take_halo(k, carry):
        halo_copy(k).wait_recv()
        for h in range(hs):
            convert(near_count + partner(k) * hs + h, rows + partner(k) * hs + h)
        return carry

    def own_halo(h, carry):
        def write(a, value):
            stage[:, a, :] = value

        for t in range(tiles):
            duplicate(outgoing[me * hs + h, :, t * LANES:(t + 1) * LANES], write, 2 * t)
        for q in range(kp):
            keep((rows + me * hs + h) * kp + q, stage[q])
        return carry

    for step in range(n_grp - 1):
        origins = (g - 1 - step, g + 1 + step)
        exists = (origins[0] >= 0, origins[1] < n_grp)
        for r in range(rows):
            for direction in range(2):
                origin = origins[direction]

                @pl.when(exists[direction])
                def _():
                    line_copy(direction, step, r, table.at[origin * rows + r], origin).wait_recv()

                if step < n_grp - 2:
                    @pl.when(exists[direction] & can_send[direction])
                    def _():
                        line_copy(direction, step + 1, r, table.at[origin * rows + r], origin).start()

            if step > 0:
                for direction in range(2):
                    @pl.when(exists[direction])
                    def _():
                        convert(origins[direction] * rows + r, direction * rows + r)
        if step == 0:
            lax.fori_loop(0, hs, own_halo, 0)
            lax.fori_loop(1, n_dom, take_halo, 0)
            multiply(g, [(g, near_index(g))] + [(n_grp + n, far_index(n)) for n in range(far_groups)])
            for s in range(len(stages)):
                if stages[s][0] < 0:
                    exchange(s)
        for direction in range(2):
            @pl.when(exists[direction])
            def _():
                if step == 0:
                    def take(r, carry):
                        convert(origins[direction] * rows + r, direction * rows + r)
                        return carry

                    lax.fori_loop(0, rows, take, 0)
                multiply(origins[direction], [(origins[direction], near_index(origins[direction]))])
        for s in range(len(stages)):
            if stages[s][0] == step:
                exchange(s)

    for s in range(len(stages)):
        collect(s)

    for r in range(owned):
        for c in range(0, kc, 2):
            value = summed[r, :, c * BS:(c + 2) * BS]
            turned = pltpu.roll(value, BS, 1)
            blocks[r, c] = jnp.where(low, value, turned)
            blocks[r, c + 1] = jnp.where(low, turned, value)

    def place_row(r, carry):
        for c in range(kc):
            blocks[owned, c] = blocks[r, plan_s[rank_at + me, hs + r, c]]
        for c in range(0, kc, SUB):
            for t in range(tiles):
                out[r, c:c + SUB, t * LANES:(t + 1) * LANES] = jnp.where(
                    low, blocks[owned, c:c + SUB, 2 * t, :], blocks[owned, c:c + SUB, 2 * t + 1, :]
                )
        return carry

    lax.fori_loop(0, owned, place_row, 0)

    def drain(k, carry):
        halo_copy(k).wait_send()
        for s in range(len(stages)):
            part_copy(s, k).wait_send()
        return carry

    lax.fori_loop(1, n_dom, drain, 0)
    for step in range(n_grp - 1):
        for r in range(rows):
            for direction in range(2):
                origin = g - step if direction == 0 else g + step
                exists = (origin >= 0) & (origin < n_grp)

                @pl.when(exists & can_send[direction])
                def _():
                    line_copy(direction, step, r, table.at[r], origin).wait_send()


def per_device(
    operator_blocks, operator_cols, halo_count, prolong_blocks, prolong_cols,
    prolong_slot, send_lists, slot_owner_row, coarse_pattern,
):
    n_grp = lax.axis_size("grp")
    n_dom = lax.axis_size("dom")
    rows, ka = operator_cols.shape
    kp = prolong_cols.shape[1]
    owned, kc = coarse_pattern.shape
    hs = send_lists.shape[1] // n_dom
    cap = slot_owner_row.shape[1] // n_dom
    total_ids = owned * n_grp * n_dom
    used = n_dom + cap - 1
    panel_count = n_grp * rows + n_dom * hs
    groups = panel_count // rows
    width = rows * BS
    plan_rows = n_grp + 3 * n_dom
    stages = ((n_grp - 2, 0, kc),)
    assert n_dom & (n_dom - 1) == 0 and (n_dom * hs) % rows == 0 and n_dom * hs >= rows
    assert kp == SUB and ka % SUB == 0 and kc % SUB == 0 and LANES % kc == 0
    assert owned < rows and kc <= ka
    assert rows % 2 == 0 and rows <= SUB and hs + owned < SUB and (owned * n_dom) % 4 == 0
    vm = lambda dtype, *shape: pltpu.VMEM(shape, dtype)
    f32, bf16, i32 = jnp.float32, jnp.bfloat16, jnp.int32
    sem = lambda *shape: pltpu.SemaphoreType.DMA(shape)
    return pl.pallas_call(
        functools.partial(fused_kernel, n_grp, n_dom, rows, hs, ka, kp, kc, cap, owned, stages),
        out_shape=jax.ShapeDtypeStruct((owned, kc, BS * BS), f32),
        in_specs=[smem_spec()] * 5 + [vmem_spec()] * 2 + [any_spec()] * 2,
        out_specs=vmem_spec(),
        scratch_shapes=[
            vm(f32, rows, kp, BS * BS), vm(f32, rows, ka, BS * BS), vm(f32, panel_count, kp, BS * BS),
            vm(f32, n_dom * hs, kp, BS * BS),
            vm(i32, SUB, LANES), vm(i32, n_grp, SUB, LANES), vm(i32, SUB, LANES),
            vm(i32, n_dom, SUB, LANES), vm(i32, n_dom, SUB, LANES),
            vm(i32, plan_rows, SUB, LANES), pltpu.SMEM((plan_rows, SUB, LANES), i32),
            vm(f32, rows, ka, BS, LANES), vm(bf16, groups, width, 2 * width),
            vm(f32, rows * kp + 1, BS, LANES), vm(f32, kp, BS, LANES),
            vm(bf16, (rows + n_dom * hs) * kp + 1, 2 * BS, LANES), vm(bf16, used, 2 * BS, width),
            vm(bf16, total_ids, width, LANES),
            vm(f32, used, BS, kc * BS), vm(f32, n_dom - 1, BS, kc * BS), vm(f32, owned, BS, kc * BS),
            sem(2), sem(2, n_grp - 1, rows), sem(2, n_grp - 1, rows), sem(n_dom), sem(n_dom),
            sem(n_grp), sem(n_grp), sem(n_dom), sem(n_dom), sem(1),
            sem(len(stages), n_dom - 1), sem(len(stages), n_dom - 1),
        ],
        compiler_params=pltpu.CompilerParams(
            collective_id=0, has_side_effects=True, vmem_limit_bytes=67043328
        ),
        name="coarse_rows",
    )(
        operator_cols, halo_count, prolong_slot, send_lists, slot_owner_row, prolong_cols, coarse_pattern,
        prolong_blocks, operator_blocks,
    )


def solution(mesh):
    blocks = P(("grp", "dom"), None, None)
    lists = P(("grp", "dom"), None)
    return jax.shard_map(
        per_device,
        mesh=mesh,
        in_specs=(blocks, lists, P(("grp", "dom")), blocks, lists, lists, lists, lists, lists),
        out_specs=blocks,
        check_vma=False,
    )
```

time: 89.8 us -> 72.8 us (0.81)
  Pallas kernels: 87.1 us -> 70.8 us
    pallas_call x3 -> x1, Pallas kernels: 87.1 us -> 70.8 us  [per_device(): pl.pallas_call(functools.partial(fused_kernel, n_grp, n_dom, rows, hs, ka...]
    reshape x1 -> x0, local copies, waits for them, and re-layouts: 2.37 us -> none  [per_device(): return summed.reshape(owned, kc, BS * BS)]
    unnamed x0 -> x1, local copies, waits for them, and re-layouts: none -> 1.87 us
where the time goes in v1:
time: 72.8 us; the launch traced here: 72.6 us
  Pallas kernels  70.8 us (97%)
  local copies, waits for them, and re-layouts  1.87 us (3%)
    pallas_call x1, Pallas kernels, per_device(): pl.pallas_call(functools.partial(fused_kernel, n_grp, n_dom, rows, hs, ka...  70.8 us
    unnamed x1, local copies, waits for them, and re-layouts  1.87 us

profile of v1, /device:TPU:0, one launch (start us, length us, event | category | flops | bytes accessed | tf_op | source)
XLA Modules:
  0.0 72.6 jit_solution(4698605853931947328)
XLA Ops:
  0.0 70.8 %coarse_rows.1 = f32[2,16,4096]{2,1,0:T(8,128)} custom-call(s32[4,16]{1,0:T(4,128)} %cols.1, s32[4]{0:T(128)} %halo.1, s32[4,8]{1,0:T(4,128)} %slots.1, s32[1,8]{1,0:T(1,128)} %picked.1, s32[1,16]{1,0:T(1,128)} %owner.1, s32[4,8]{1,0:T(4,128)} %prolong_cols.1, s32[2,16]{1,0:T(2,128)} %pattern.1, f32[4,8,4096]{2,1,0:T(8,128)} %prolong_in.1, ...), custom_call_target="tpu_custom_call" | custom-call | tf_op jit(solution)/shard_map/coarse_rows/pallas_call | solution.py:519
  70.8 1.9 %copy.11 = f32[2,16,4096]{2,1,0:T(8,128)} copy(f32[2,16,4096]{2,1,0:T(8,128)} %coarse_rows.1) | data formatting | bytes 1048576

commit v2 on v1

--- a/solution.py
+++ b/solution.py
@@ -28,11 +28,12 @@
 def fused_kernel(
     n_grp, n_dom, rows, hs, ka, kp, kc, cap, owned, stages,
     cols, halo, slots, picked, owner, prolong_cols, pattern, prolong_in, operator_in,
-    out,
+    out, late,
     own_raw, operator, table, outgoing, grp_out, grp_in, dom_base, dom_out, dom_in, plan_v, plan_s,
     blocks, dense, own_dup, stage, panels, left, ap, partial, arrived, summed,
     load_sem, line_send, line_recv, halo_send, halo_recv,
     gmeta_send, gmeta_recv, dmeta_send, dmeta_recv, plan_sem, part_send, part_recv,
+    late_out, late_in, late_send, late_recv,
 ):
     g = lax.axis_index("grp")
     me = lax.axis_index("dom")
@@ -243,13 +244,16 @@
 
     slot_of_lane = lax.rem(lane, kc)
 
-    def dom_tables(d, carry):
+    pattern_line = (sub >= hs) & (sub < hs + owned)
+
+    def dom_tables(d, wrong):
         values = dom_in[d]
         plan_v[n_grp + d] = places(values, g * plane_ids, rows + d * hs)
         plane = jnp.zeros((SUB, LANES), jnp.int32)
         for n in range(1, n_grp):
             plane += (values >= n * plane_ids).astype(jnp.int32)
-        order = jnp.abs(plane - g) * kc + slot_of_lane
+        distance = jnp.abs(plane - g)
+        order = distance * kc + slot_of_lane
         rank = jnp.zeros((SUB, LANES), jnp.int32)
         for s in range(1, kc):
             rank += (pltpu.roll(order, s, 1) < order).astype(jnp.int32)
@@ -258,11 +262,22 @@
             ordered = jnp.where(pltpu.roll(rank, s, 1) == slot_of_lane, pltpu.roll(values, s, 1), ordered)
         plan_v[sort_at + d] = ordered
         plan_v[rank_at + d] = rank
-        return carry
-
-    lax.fori_loop(0, n_dom, dom_tables, 0)
+        for after, _, last in stages:
+            wrong |= (pattern_line & (rank < last) & (distance > after + 1)).astype(jnp.int32)
+        return wrong
+
+    wrong = lax.fori_loop(0, n_dom, dom_tables, jnp.zeros((SUB, LANES), jnp.int32))
     plan_copy = pltpu.make_async_copy(plan_v, plan_s, plan_sem.at[0])
     plan_copy.start()
+    late_out[...] = wrong
+    late_in[g] = wrong
+
+    def late_copy(k):
+        return pltpu.make_async_remote_copy(
+            src_ref=late_out, dst_ref=late_in.at[g], send_sem=late_send.at[k], recv_sem=late_recv.at[k],
+            device_id={"grp": lax.rem(g + k, n_grp)},
+        )
+
 
     def transposed(slot, at):
         for pair in range(0, rows, 2):
@@ -282,6 +297,8 @@
         return carry
 
     lax.fori_loop(1, n_dom, far_left, 0)
+    for k in range(1, n_grp):
+        late_copy(k).start()
     for t in range(cap):
         transposed(me * cap + t, 0 if t == 0 else n_dom + t - 1)
 
@@ -451,6 +468,13 @@
             if stages[s][0] == step:
                 exchange(s)
 
+    for k in range(1, n_grp):
+        late_copy(k).wait()
+    anywhere = late_in[0]
+    for k in range(1, n_grp):
+        anywhere |= late_in[k]
+    late[...] = jnp.broadcast_to(jnp.max(jnp.max(anywhere, axis=0, keepdims=True), axis=1, keepdims=True), (SUB, LANES))
+
     for s in range(len(stages)):
         collect(s)
 
@@ -508,7 +532,10 @@
     groups = panel_count // rows
     width = rows * BS
     plan_rows = n_grp + 3 * n_dom
-    stages = ((n_grp - 2, 0, kc),)
+    quarter, half = kc // 4, kc // 2
+    at_once = ((n_grp - 2, 0, kc),)
+    by_distance = ((n_grp - 4, 0, quarter), (n_grp - 3, quarter, half), (n_grp - 2, half, kc))
+    assert n_grp >= 3 and quarter % 2 == 0
     assert n_dom & (n_dom - 1) == 0 and (n_dom * hs) % rows == 0 and n_dom * hs >= rows
     assert kp == SUB and ka % SUB == 0 and kc % SUB == 0 and LANES % kc == 0
     assert owned < rows and kc <= ka
@@ -516,11 +543,11 @@
     vm = lambda dtype, *shape: pltpu.VMEM(shape, dtype)
     f32, bf16, i32 = jnp.float32, jnp.bfloat16, jnp.int32
     sem = lambda *shape: pltpu.SemaphoreType.DMA(shape)
-    return pl.pallas_call(
+    call = lambda stages, number, name: pl.pallas_call(
         functools.partial(fused_kernel, n_grp, n_dom, rows, hs, ka, kp, kc, cap, owned, stages),
-        out_shape=jax.ShapeDtypeStruct((owned, kc, BS * BS), f32),
+        out_shape=(jax.ShapeDtypeStruct((owned, kc, BS * BS), f32), jax.ShapeDtypeStruct((SUB, LANES), i32)),
         in_specs=[smem_spec()] * 5 + [vmem_spec()] * 2 + [any_spec()] * 2,
-        out_specs=vmem_spec(),
+        out_specs=(vmem_spec(), vmem_spec()),
         scratch_shapes=[
             vm(f32, rows, kp, BS * BS), vm(f32, rows, ka, BS * BS), vm(f32, panel_count, kp, BS * BS),
             vm(f32, n_dom * hs, kp, BS * BS),
@@ -535,15 +562,19 @@
             sem(2), sem(2, n_grp - 1, rows), sem(2, n_grp - 1, rows), sem(n_dom), sem(n_dom),
             sem(n_grp), sem(n_grp), sem(n_dom), sem(n_dom), sem(1),
             sem(len(stages), n_dom - 1), sem(len(stages), n_dom - 1),
+            vm(i32, SUB, LANES), vm(i32, n_grp, SUB, LANES), sem(n_grp), sem(n_grp),
         ],
         compiler_params=pltpu.CompilerParams(
-            collective_id=0, has_side_effects=True, vmem_limit_bytes=67043328
+            collective_id=number, has_side_effects=True, vmem_limit_bytes=67043328
         ),
-        name="coarse_rows",
-    )(
+        name=name,
+    )
+    args = (
         operator_cols, halo_count, prolong_slot, send_lists, slot_owner_row, prolong_cols, coarse_pattern,
         prolong_blocks, operator_blocks,
     )
+    result, late = call(by_distance, 0, "coarse_rows")(*args)
+    return lax.cond(late[0, 0] > 0, lambda: call(at_once, 1, "coarse_rows_at_once")(*args)[0], lambda: result)
 
 
 def solution(mesh):

time: 72.8 us -> 66.1 us (0.908)
  Pallas kernels: 70.8 us -> 61.9 us
  local copies, waits for them, and re-layouts: 1.87 us -> 3.07 us
    pallas_call x1, Pallas kernels: 70.8 us -> 61.9 us  [per_device(): result, late = call(by_distance, 0, 'coarse_rows')(*args)]
    slice x0 -> x1, local copies, waits for them, and re-layouts: none -> 1.2 us  [per_device(): late[0, 0] > 0]
where the time goes in v2:
time: 66.1 us; the launch traced here: 65.9 us
  Pallas kernels  61.9 us (94%)
  local copies, waits for them, and re-layouts  3.07 us (5%)
  between operations  0.67 us (1%)
    pallas_call x1, Pallas kernels, per_device(): result, late = call(by_distance, 0, 'coarse_rows')(*args)  61.9 us
    unnamed x1, local copies, waits for them, and re-layouts  1.87 us

profile of v2, /device:TPU:0, one launch (start us, length us, event | category | flops | bytes accessed | tf_op | source)
XLA Modules:
  0.0 65.9 jit_solution(303348925751831847)
XLA Ops:
  0.0 61.9 %coarse_rows.1 = (f32[2,16,4096]{2,1,0:T(8,128)}, s32[8,128]{1,0:T(8,128)}) custom-call(s32[4,16]{1,0:T(4,128)} %cols.1, s32[4]{0:T(128)} %halo.1, s32[4,8]{1,0:T(4,128)} %slots.1, s32[1,8]{1,0:T(1,128)} %picked.1, s32[1,16]{1,0:T(1,128)} %owner.1, s32[4,8]{1,0:T(4,128)} %prolong_cols.1, s32[2,16]{1,0:T(2,128)} %pattern.1, f32[4,8,4096]{2,1,0:T(8,128)} %prolong_in.1, ...), custom_call_target="tpu_custom_call" | custom-call | tf_op jit(solution)/shard_map/coarse_rows/pallas_call | solution.py:576
  62.0 1.2 %slice.3 = s32[1,1]{1,0:T(1,128)} slice(s32[8,128]{1,0:T(8,128)} %get-tuple-element.39), slice={[0:1], [0:1]} | slice | bytes 8 | tf_op jit(solution)/shard_map/slice | solution.py:577
  63.8 0.2 conditional.1
  64.0 1.9 %copy.15 = f32[2,16,4096]{2,1,0:T(8,128)} copy(f32[2,16,4096]{2,1,0:T(8,128)} %get-tuple-element.41) | data formatting | bytes 1048576

commit v3 on v2

--- a/solution.py
+++ b/solution.py
@@ -309,7 +309,7 @@
     lax.fori_loop(0, rows * kp, own_panels, 0)
     plan_copy.wait()
 
-    def multiply(plane, parts):
+    def multiply(plane, parts, used_rows=range(rows), saved=None, last=True):
         def four(n, carry):
             e = n * 4
             total = None
@@ -318,18 +318,25 @@
                 for pair in range(2):
                     blocks_here = [
                         jnp.where(low, panels[index_of(r, e + 2 * pair)], panels[index_of(r, e + 2 * pair + 1)])
-                        for r in range(rows)
+                        for r in used_rows
                     ]
                     high = [b[0:BS] for b in blocks_here]
                     rest = [b[BS:2 * BS] for b in blocks_here]
                     halves.append(jnp.concatenate(high + rest + high, axis=0))
                 right = jnp.concatenate(halves, axis=1)
-                split_dense = dense[group]
-                lhs = jnp.concatenate([split_dense[:, 0:width], split_dense], axis=1)
+                first, depth = used_rows[0] * BS, len(used_rows) * BS
+                lhs_high = dense[group, :, first:first + depth]
+                lhs = jnp.concatenate([lhs_high, lhs_high, dense[group, :, width + first:width + first + depth]], axis=1)
                 product = jnp.dot(lhs, right, preferred_element_type=jnp.float32)
                 total = product if total is None else total + product
             for pair in range(2):
                 value = total[:, pair * LANES:(pair + 1) * LANES]
+                if not last:
+                    for i in range(rows):
+                        blocks[i, saved + 2 * n + pair] = value[i * BS:(i + 1) * BS]
+                    continue
+                if saved is not None:
+                    value += jnp.concatenate([blocks[i, saved + 2 * n + pair] for i in range(rows)], axis=0)
                 high = value.astype(jnp.bfloat16).astype(jnp.float32)
                 rest = value - high
                 turned = pltpu.roll(jnp.where(low, rest, high), BS, 1)
@@ -426,6 +433,7 @@
             keep((rows + me * hs + h) * kp + q, stage[q])
         return carry
 
+    in_halves = plane_ids <= ka and rows % 4 == 0
     for step in range(n_grp - 1):
         origins = (g - 1 - step, g + 1 + step)
         exists = (origins[0] >= 0, origins[1] < n_grp)
@@ -447,6 +455,11 @@
                     @pl.when(exists[direction])
                     def _():
                         convert(origins[direction] * rows + r, direction * rows + r)
+                        if in_halves and r == rows // 2 - 1:
+                            multiply(
+                                origins[direction], [(origins[direction], near_index(origins[direction]))],
+                                range(rows // 2), direction * plane_ids // 2, False,
+                            )
         if step == 0:
             lax.fori_loop(0, hs, own_halo, 0)
             lax.fori_loop(1, n_dom, take_halo, 0)
@@ -463,7 +476,11 @@
                         return carry
 
                     lax.fori_loop(0, rows, take, 0)
-                multiply(origins[direction], [(origins[direction], near_index(origins[direction]))])
+                parts = [(origins[direction], near_index(origins[direction]))]
+                if step > 0 and in_halves:
+                    multiply(origins[direction], parts, range(rows // 2, rows), direction * plane_ids // 2)
+                else:
+                    multiply(origins[direction], parts)
         for s in range(len(stages)):
             if stages[s][0] == step:
                 exchange(s)
@@ -473,7 +490,7 @@
     anywhere = late_in[0]
     for k in range(1, n_grp):
         anywhere |= late_in[k]
-    late[...] = jnp.broadcast_to(jnp.max(jnp.max(anywhere, axis=0, keepdims=True), axis=1, keepdims=True), (SUB, LANES))
+    late[...] = jnp.max(jnp.max(anywhere, axis=0, keepdims=True), axis=1, keepdims=True)
 
     for s in range(len(stages)):
         collect(s)
@@ -545,7 +562,9 @@
     sem = lambda *shape: pltpu.SemaphoreType.DMA(shape)
     call = lambda stages, number, name: pl.pallas_call(
         functools.partial(fused_kernel, n_grp, n_dom, rows, hs, ka, kp, kc, cap, owned, stages),
-        out_shape=(jax.ShapeDtypeStruct((owned, kc, BS * BS), f32), jax.ShapeDtypeStruct((SUB, LANES), i32)),
+        out_shape=(
+            jax.ShapeDtypeStruct((owned, kc, BS * BS), f32), jax.ShapeDtypeStruct((1, 1), i32),
+        ),
         in_specs=[smem_spec()] * 5 + [vmem_spec()] * 2 + [any_spec()] * 2,
         out_specs=(vmem_spec(), vmem_spec()),
         scratch_shapes=[
@@ -574,7 +593,8 @@
         prolong_blocks, operator_blocks,
     )
     result, late = call(by_distance, 0, "coarse_rows")(*args)
-    return lax.cond(late[0, 0] > 0, lambda: call(at_once, 1, "coarse_rows_at_once")(*args)[0], lambda: result)
+    result = lax.cond(late.reshape(()) > 0, lambda: call(at_once, 1, "coarse_rows_at_once")(*args)[0], lambda: result)
+    return result
 
 
 def solution(mesh):

time: 66.1 us -> 64.5 us (0.976)
  local copies, waits for them, and re-layouts: 3.07 us -> 1.87 us
    slice x1 -> x0, local copies, waits for them, and re-layouts: 1.2 us -> none  [per_device(): late[0, 0] > 0]
where the time goes in v3:
time: 64.5 us; the launch traced here: 64.3 us
  Pallas kernels  61.7 us (96%)
  local copies, waits for them, and re-layouts  1.87 us (3%)
    pallas_call x1, Pallas kernels, per_device(): result, late = call(by_distance, 0, 'coarse_rows')(*args)  61.7 us
    unnamed x1, local copies, waits for them, and re-layouts  1.87 us

profile of v3, /device:TPU:0, one launch (start us, length us, event | category | flops | bytes accessed | tf_op | source)
XLA Modules:
  0.0 64.3 jit_solution(5470452393125760470)
XLA Ops:
  0.0 61.7 %coarse_rows.1 = (f32[2,16,4096]{2,1,0:T(8,128)}, s32[1,1]{1,0:T(1,128)}) custom-call(s32[4,16]{1,0:T(4,128)} %cols.1, s32[4]{0:T(128)} %halo.1, s32[4,8]{1,0:T(4,128)} %slots.1, s32[1,8]{1,0:T(1,128)} %picked.1, s32[1,16]{1,0:T(1,128)} %owner.1, s32[4,8]{1,0:T(4,128)} %prolong_cols.1, s32[2,16]{1,0:T(2,128)} %pattern.1, f32[4,8,4096]{2,1,0:T(8,128)} %prolong_in.1, ...), custom_call_target="tpu_custom_call" | custom-call | tf_op jit(solution)/shard_map/coarse_rows/pallas_call | solution.py:595
  62.2 0.2 conditional.1
  62.5 1.9 %copy.15 = f32[2,16,4096]{2,1,0:T(8,128)} copy(f32[2,16,4096]{2,1,0:T(8,128)} %get-tuple-element.41) | data formatting | bytes 1048576

commit v4 on v3

--- a/solution.py
+++ b/solution.py
@@ -26,7 +26,7 @@
 
 
 def fused_kernel(
-    n_grp, n_dom, rows, hs, ka, kp, kc, cap, owned, stages,
+    n_grp, n_dom, rows, hs, ka, kp, kc, cap, owned, stages, merge,
     cols, halo, slots, picked, owner, prolong_cols, pattern, prolong_in, operator_in,
     out, late,
     own_raw, operator, table, outgoing, grp_out, grp_in, dom_base, dom_out, dom_in, plan_v, plan_s,
@@ -34,6 +34,7 @@
     load_sem, line_send, line_recv, halo_send, halo_recv,
     gmeta_send, gmeta_recv, dmeta_send, dmeta_recv, plan_sem, part_send, part_recv,
     late_out, late_in, late_send, late_recv,
+    feed, merged, merged_in, source_row, feed_send, feed_recv, merged_send, merged_recv,
 ):
     g = lax.axis_index("grp")
     me = lax.axis_index("dom")
@@ -76,6 +77,12 @@
         for j in range(0, LANES, kc):
             dom_base[hs + r:hs + r + 1, j:j + kc] = pattern[r:r + 1, :]
 
+    if merge:
+        line = jnp.zeros((1, LANES), jnp.int32)
+        for t in range(n_dom * cap):
+            line = jnp.where(lane[0:1] == t, owner[0, t], line)
+        dom_base[row_at + 1:row_at + 2, :] = line
+
     def for_dom(d, carry):
         dom_out[d] = dom_base[...]
         for h in range(hs):
@@ -94,6 +101,8 @@
             send_sem=line_send.at[direction, step, r], recv_sem=line_recv.at[direction, step, r],
             device_id={"grp": g + 1 if direction == 0 else g - 1},
         )
+
+    merge_sources = ((2, 3, 1, 0), (4, 5, 1, 0))
 
     def grp_meta(k):
         return pltpu.make_async_remote_copy(
@@ -265,6 +274,14 @@
         for after, _, last in stages:
             wrong |= (pattern_line & (rank < last) & (distance > after + 1)).astype(jnp.int32)
         return wrong
+
+    if merge:
+        for way in range(2):
+            goal = partner(4 if way == 0 else 2) * cap
+            for n, source in enumerate(merge_sources[way]):
+                found = jnp.where(lane[0:1] == goal, dom_in[partner(source), row_at + 1:row_at + 2, :], 0)
+                splat = jnp.broadcast_to(jnp.sum(found, axis=1, keepdims=True), (1, LANES))
+                source_row[4 * way + n:4 * way + n + 1, :] = splat
 
     wrong = lax.fori_loop(0, n_dom, dom_tables, jnp.zeros((SUB, LANES), jnp.int32))
     plan_copy = pltpu.make_async_copy(plan_v, plan_s, plan_sem.at[0])
@@ -356,8 +373,8 @@
             return plan_s[n_grp + n // hs, n % hs, e]
         return index_of
 
-    def part_copy(s, k):
-        first, last = stages[s][1:]
+    def part_copy(s, k, window=None):
+        first, last = stages[s][1:] if window is None else window
         here = pl.ds(first * BS, (last - first) * BS)
         return pltpu.make_async_remote_copy(
             src_ref=partial.at[k, :, here], dst_ref=arrived.at[k - 1, :, here],
@@ -376,8 +393,9 @@
             partial[at, :, c * BS:(c + 2) * BS] = jnp.where(low, one, two) + pltpu.roll(jnp.where(low, two, one), BS, 1)
 
     def exchange(s):
-        first, last = stages[s][1:]
-        here = slice(first * BS, last * BS)
+        if merge and s == len(stages) - 1:
+            exchange_merged()
+            return
 
         def far_slot(step, carry):
             k = n_dom - step
@@ -391,8 +409,14 @@
             return carry
 
         lax.fori_loop(1, n_dom, far_slot, 0)
+        own_slots(s, lambda: part_copy(s, 1).start())
+
+    def own_slots(s, then=None):
+        first, last = stages[s][1:]
+        here = slice(first * BS, last * BS)
         slot_rows(s, me, me * cap, 0)
-        part_copy(s, 1).start()
+        if then is not None:
+            then()
         for t in range(1, cap):
             slot_rows(s, me, me * cap + t, n_dom + t - 1)
         for r in range(owned):
@@ -402,6 +426,9 @@
             summed[r, :, here] = total
 
     def collect(s):
+        if merge and s == len(stages) - 1:
+            collect_merged()
+            return
         first, last = stages[s][1:]
 
         def one(step, carry):
@@ -416,6 +443,86 @@
             return carry
 
         lax.fori_loop(1, n_dom, one, 0)
+
+    def way_window(way):
+        first, last = stages[-1][1:]
+        middle = (first + last) // 2
+        return (first, middle) if way == 0 else (middle, last)
+
+    def feed_copy(k, way, to, place):
+        first, last = way_window(way)
+        return pltpu.make_async_remote_copy(
+            src_ref=partial.at[k, :, pl.ds(first * BS, (last - first) * BS)], dst_ref=feed.at[way, place],
+            send_sem=feed_send.at[way, place], recv_sem=feed_recv.at[way, place],
+            device_id={"dom": partner(to)},
+        )
+
+    def merged_copy(way):
+        return pltpu.make_async_remote_copy(
+            src_ref=merged.at[way], dst_ref=merged_in.at[way], send_sem=merged_send.at[way], recv_sem=merged_recv.at[way],
+            device_id={"dom": partner(4 if way == 0 else 2)},
+        )
+
+    def feeds_of(k):
+        if k > 5:
+            return [feed_copy(k, 0, k - 4, k - 6), feed_copy(k, 1, k - 2, k - 6)]
+        if k == 5:
+            return [feed_copy(k, 0, 1, 2)]
+        return [feed_copy(k, 1, 1, 2)] if k == 3 else []
+
+    def direct_of(k):
+        s = len(stages) - 1
+        if k == 1:
+            return [part_copy(s, k)]
+        return [part_copy(s, k, way_window(0 if k < 4 else 1))] if k < 6 else []
+
+    def exchange_merged():
+        s = len(stages) - 1
+        before = None
+        for k in (7, 6, 5, 3, 4, 2, 1):
+            slot_rows(s, partner(k), partner(k) * cap, k)
+            if before is not None:
+                for copy in feeds_of(before) + direct_of(before):
+                    copy.start()
+            before = k
+        own_slots(s)
+        for copy in feeds_of(before) + direct_of(before):
+            copy.start()
+        for way in range(2):
+            window = way_window(way)
+            for k in (7, 6, 5 if way == 0 else 3):
+                feeds_of(k)[way if k > 5 else 0].wait_recv()
+            for c in range(window[0], window[1], 2):
+                here = slice((c - window[0]) * BS, (c - window[0] + 2) * BS)
+                values = [feed[way, n, :, here] for n in range(3)]
+                values.append(partial[4 if way == 0 else 2, :, c * BS:(c + 2) * BS])
+                for r in range(owned):
+                    total = None
+                    for n in range(4):
+                        term = jnp.where(source_row[4 * way + n:4 * way + n + 1, :] == r, values[n], 0.0)
+                        total = term if total is None else total + term
+                    merged[way, r, :, here] = total
+        for way in range(2):
+            merged_copy(way).start()
+
+    def add_rows(row, values_of, window):
+        for c in range(window[0], window[1], 2):
+            here = slice(c * BS, (c + 2) * BS)
+            value = values_of(here)
+            for r in range(owned):
+                summed[r, :, here] += jnp.where(row == r, value, 0.0)
+
+    def collect_merged():
+        first, last = stages[-1][1:]
+        for k in (1, 3, 2, 5, 4):
+            direct_of(k)[0].wait_recv()
+            window = (first, last) if k == 1 else way_window(0 if k < 4 else 1)
+            add_rows(dom_in[partner(k), row_at:row_at + 1, :], lambda here: arrived[k - 1, :, here], window)
+        for way in range(2):
+            merged_copy(way).wait_recv()
+            first, last = way_window(way)
+            for r in range(owned):
+                summed[r, :, first * BS:last * BS] += merged_in[way, r]
 
     def take_halo(k, carry):
         halo_copy(k).wait_recv()
@@ -516,11 +623,17 @@
 
     def drain(k, carry):
         halo_copy(k).wait_send()
-        for s in range(len(stages)):
+        for s in range(len(stages) - int(merge)):
             part_copy(s, k).wait_send()
         return carry
 
     lax.fori_loop(1, n_dom, drain, 0)
+    if merge:
+        for k in range(1, n_dom):
+            for copy in feeds_of(k) + direct_of(k):
+                copy.wait_send()
+        for way in range(2):
+            merged_copy(way).wait_send()
     for step in range(n_grp - 1):
         for r in range(rows):
             for direction in range(2):
@@ -553,6 +666,8 @@
     at_once = ((n_grp - 2, 0, kc),)
     by_distance = ((n_grp - 4, 0, quarter), (n_grp - 3, quarter, half), (n_grp - 2, half, kc))
     assert n_grp >= 3 and quarter % 2 == 0
+    part = quarter * BS
+    through_chip = n_dom == 8 and hs + owned + 2 <= SUB and n_dom * cap <= LANES
     assert n_dom & (n_dom - 1) == 0 and (n_dom * hs) % rows == 0 and n_dom * hs >= rows
     assert kp == SUB and ka % SUB == 0 and kc % SUB == 0 and LANES % kc == 0
     assert owned < rows and kc <= ka
@@ -560,8 +675,8 @@
     vm = lambda dtype, *shape: pltpu.VMEM(shape, dtype)
     f32, bf16, i32 = jnp.float32, jnp.bfloat16, jnp.int32
     sem = lambda *shape: pltpu.SemaphoreType.DMA(shape)
-    call = lambda stages, number, name: pl.pallas_call(
-        functools.partial(fused_kernel, n_grp, n_dom, rows, hs, ka, kp, kc, cap, owned, stages),
+    call = lambda stages, merge, number, name: pl.pallas_call(
+        functools.partial(fused_kernel, n_grp, n_dom, rows, hs, ka, kp, kc, cap, owned, stages, merge),
         out_shape=(
             jax.ShapeDtypeStruct((owned, kc, BS * BS), f32), jax.ShapeDtypeStruct((1, 1), i32),
         ),
@@ -582,6 +697,8 @@
             sem(n_grp), sem(n_grp), sem(n_dom), sem(n_dom), sem(1),
             sem(len(stages), n_dom - 1), sem(len(stages), n_dom - 1),
             vm(i32, SUB, LANES), vm(i32, n_grp, SUB, LANES), sem(n_grp), sem(n_grp),
+            vm(f32, 2, 3, BS, part if merge else LANES), vm(f32, 2, owned, BS, part if merge else LANES),
+            vm(f32, 2, owned, BS, part if merge else LANES), vm(i32, SUB, LANES), sem(2, 3), sem(2, 3), sem(2), sem(2),
         ],
         compiler_params=pltpu.CompilerParams(
             collective_id=number, has_side_effects=True, vmem_limit_bytes=67043328
@@ -592,8 +709,8 @@
         operator_cols, halo_count, prolong_slot, send_lists, slot_owner_row, prolong_cols, coarse_pattern,
         prolong_blocks, operator_blocks,
     )
-    result, late = call(by_distance, 0, "coarse_rows")(*args)
-    result = lax.cond(late.reshape(()) > 0, lambda: call(at_once, 1, "coarse_rows_at_once")(*args)[0], lambda: result)
+    result, late = call(by_distance, through_chip, 0, "coarse_rows")(*args)
+    result = lax.cond(late.reshape(()) > 0, lambda: call(at_once, False, 1, "coarse_rows_at_once")(*args)[0], lambda: result)
     return result
 
 

time: 64.5 us -> 61.5 us (0.953)
  Pallas kernels: 61.7 us -> 58.7 us
    pallas_call x1, Pallas kernels: 61.7 us -> 58.7 us  [per_device(): result, late = call(by_distance, through_chip, 0, 'coarse_rows')(*args)]
where the time goes in v4:
time: 61.5 us; the launch traced here: 61.4 us
  Pallas kernels  58.7 us (95%)
  local copies, waits for them, and re-layouts  1.87 us (3%)
    pallas_call x1, Pallas kernels, per_device(): result, late = call(by_distance, through_chip, 0, 'coarse_rows')(*args)  58.7 us
    unnamed x1, local copies, waits for them, and re-layouts  1.87 us

profile of v4, /device:TPU:0, one launch (start us, length us, event | category | flops | bytes accessed | tf_op | source)
XLA Modules:
  0.0 61.4 jit_solution(18000639245520429659)
XLA Ops:
  0.0 58.7 %coarse_rows.1 = (f32[2,16,4096]{2,1,0:T(8,128)}, s32[1,1]{1,0:T(1,128)}) custom-call(s32[4,16]{1,0:T(4,128)} %cols.1, s32[4]{0:T(128)} %halo.1, s32[4,8]{1,0:T(4,128)} %slots.1, s32[1,8]{1,0:T(1,128)} %picked.1, s32[1,16]{1,0:T(1,128)} %owner.1, s32[4,8]{1,0:T(4,128)} %prolong_cols.1, s32[2,16]{1,0:T(2,128)} %pattern.1, f32[4,8,4096]{2,1,0:T(8,128)} %prolong_in.1, ...), custom_call_target="tpu_custom_call" | custom-call | tf_op jit(solution)/shard_map/coarse_rows/pallas_call | solution.py:712
  59.2 0.2 conditional.1
  59.5 1.9 %copy.15 = f32[2,16,4096]{2,1,0:T(8,128)} copy(f32[2,16,4096]{2,1,0:T(8,128)} %get-tuple-element.41) | data formatting | bytes 1048576

commit v5 on v4

--- a/solution.py
+++ b/solution.py
@@ -1,4 +1,5 @@
 import functools
+import math
 
 import jax
 import jax.numpy as jnp
@@ -11,6 +12,8 @@
 KG = 12
 LANES = 128
 SUB = 8
+MOST_VMEM = 67043328
+SPARE = 6 << 20
 
 
 def any_spec():
@@ -675,14 +678,8 @@
     vm = lambda dtype, *shape: pltpu.VMEM(shape, dtype)
     f32, bf16, i32 = jnp.float32, jnp.bfloat16, jnp.int32
     sem = lambda *shape: pltpu.SemaphoreType.DMA(shape)
-    call = lambda stages, merge, number, name: pl.pallas_call(
-        functools.partial(fused_kernel, n_grp, n_dom, rows, hs, ka, kp, kc, cap, owned, stages, merge),
-        out_shape=(
-            jax.ShapeDtypeStruct((owned, kc, BS * BS), f32), jax.ShapeDtypeStruct((1, 1), i32),
-        ),
-        in_specs=[smem_spec()] * 5 + [vmem_spec()] * 2 + [any_spec()] * 2,
-        out_specs=(vmem_spec(), vmem_spec()),
-        scratch_shapes=[
+    def call(stages, merge, number, name):
+        scratch = [
             vm(f32, rows, kp, BS * BS), vm(f32, rows, ka, BS * BS), vm(f32, panel_count, kp, BS * BS),
             vm(f32, n_dom * hs, kp, BS * BS),
             vm(i32, SUB, LANES), vm(i32, n_grp, SUB, LANES), vm(i32, SUB, LANES),
@@ -699,16 +696,27 @@
             vm(i32, SUB, LANES), vm(i32, n_grp, SUB, LANES), sem(n_grp), sem(n_grp),
             vm(f32, 2, 3, BS, part if merge else LANES), vm(f32, 2, owned, BS, part if merge else LANES),
             vm(f32, 2, owned, BS, part if merge else LANES), vm(i32, SUB, LANES), sem(2, 3), sem(2, 3), sem(2), sem(2),
-        ],
-        compiler_params=pltpu.CompilerParams(
-            collective_id=number, has_side_effects=True, vmem_limit_bytes=67043328
-        ),
-        name=name,
-    )
+        ]
+        held = sum(math.prod(x.shape) * x.dtype.itemsize for x in scratch if x.memory_space == pltpu.VMEM)
+        return pl.pallas_call(
+            functools.partial(fused_kernel, n_grp, n_dom, rows, hs, ka, kp, kc, cap, owned, stages, merge),
+            out_shape=(
+                jax.ShapeDtypeStruct((owned, kc, BS * BS), f32), jax.ShapeDtypeStruct((1, 1), i32),
+            ),
+            in_specs=[smem_spec()] * 5 + [vmem_spec()] * 2 + [any_spec()] * 2,
+            out_specs=(vmem_spec(), vmem_spec()),
+            scratch_shapes=scratch,
+            compiler_params=pltpu.CompilerParams(
+                collective_id=number, has_side_effects=True, vmem_limit_bytes=min(held + SPARE, MOST_VMEM)
+            ),
+            name=name,
+        )
+
     args = (
         operator_cols, halo_count, prolong_slot, send_lists, slot_owner_row, prolong_cols, coarse_pattern,
         prolong_blocks, operator_blocks,
     )
+    args = tuple(pltpu.with_memory_space_constraint(x, pltpu.HBM) for x in args)
     result, late = call(by_distance, through_chip, 0, "coarse_rows")(*args)
     result = lax.cond(late.reshape(()) > 0, lambda: call(at_once, False, 1, "coarse_rows_at_once")(*args)[0], lambda: result)
     return result

time: 61.5 us -> 60.2 us (0.979)
  local copies, waits for them, and re-layouts: 1.87 us -> 0.8 us
    unnamed x1, local copies, waits for them, and re-layouts: 1.87 us -> 0.8 us
where the time goes in v5:
time: 60.2 us; the launch traced here: 60.1 us
  Pallas kernels  58.4 us (97%)
  local copies, waits for them, and re-layouts  0.8 us (1%)
  between operations  0.63 us (1%)
    pallas_call x1, Pallas kernels, per_device(): result, late = call(by_distance, through_chip, 0, 'coarse_rows')(*args)  58.4 us

profile of v5, /device:TPU:0, one launch (start us, length us, event | category | flops | bytes accessed | tf_op | source)
XLA Modules:
  0.0 60.1 jit_solution(5244043280316616460)
XLA Ops:
  0.0 58.4 %coarse_rows.1 = (f32[2,16,4096]{2,1,0:T(8,128)S(1)}, s32[1,1]{1,0:T(1,128)}) custom-call(s32[4,16]{1,0:T(4,128)} %cols.1, s32[4]{0:T(128)} %halo.1, s32[4,8]{1,0:T(4,128)} %slots.1, s32[1,8]{1,0:T(1,128)} %picked.1, s32[1,16]{1,0:T(1,128)} %owner.1, s32[4,8]{1,0:T(4,128)} %prolong_cols.1, s32[2,16]{1,0:T(2,128)} %pattern.1, f32[4,8,4096]{2,1,0:T(8,128)} %prolong_in.1, ...), custom_call_target="tpu_custom_call" | custom-call | tf_op jit(solution)/shard_map/coarse_rows/pallas_call | solution.py:720
  59.0 0.2 conditional.1
  59.3 0.8 %copy.15 = f32[2,16,4096]{2,1,0:T(8,128)} copy(f32[2,16,4096]{2,1,0:T(8,128)S(1)} %get-tuple-element.41) | data formatting | bytes 1048576

commit v6 on v5

--- a/solution.py
+++ b/solution.py
@@ -73,6 +73,47 @@
             bit *= 2
         return other
 
+    pl.semaphore_wait(barrier, n_grp + n_dom - 2)
+
+    def line_copy(direction, step, r, src, origin):
+        return pltpu.make_async_remote_copy(
+            src_ref=src, dst_ref=table.at[origin * rows + r],
+            send_sem=line_send.at[direction, step, r], recv_sem=line_recv.at[direction, step, r],
+            device_id={"grp": g + 1 if direction == 0 else g - 1},
+        )
+
+    merge_sources = ((2, 3, 1, 0), (4, 5, 1, 0))
+
+    def grp_meta(k):
+        return pltpu.make_async_remote_copy(
+            src_ref=grp_out, dst_ref=grp_in.at[g], send_sem=gmeta_send.at[k], recv_sem=gmeta_recv.at[k],
+            device_id={"grp": lax.rem(g + k, n_grp)},
+        )
+
+    def dom_meta(k):
+        target = partner(k)
+        return pltpu.make_async_remote_copy(
+            src_ref=dom_out.at[target], dst_ref=dom_in.at[me], send_sem=dmeta_send.at[k], recv_sem=dmeta_recv.at[k],
+            device_id={"dom": target},
+        )
+
+    def halo_copy(k):
+        target = partner(k)
+        return pltpu.make_async_remote_copy(
+            src_ref=outgoing.at[pl.ds(target * hs, hs)], dst_ref=table.at[pl.ds(near_count + me * hs, hs)],
+            send_sem=halo_send.at[k], recv_sem=halo_recv.at[k],
+            device_id={"dom": target},
+        )
+
+    can_send = (g < n_grp - 1, g > 0)
+
+    def send_own(r):
+        for direction in range(2):
+            @pl.when(can_send[direction])
+            def _():
+                line_copy(direction, 0, r, prolong_in.at[r], g).start()
+
+    send_own(0)
     grp_out[...] = jnp.zeros(grp_out.shape, jnp.int32)
     grp_out[0:rows, 0:kp] = prolong_cols[...]
     dom_base[...] = jnp.zeros(dom_base.shape, jnp.int32)
@@ -96,38 +137,6 @@
     lax.fori_loop(0, n_dom, for_dom, 0)
     grp_in[g] = grp_out[...]
     dom_in[me] = dom_out[me]
-    pl.semaphore_wait(barrier, n_grp + n_dom - 2)
-
-    def line_copy(direction, step, r, src, origin):
-        return pltpu.make_async_remote_copy(
-            src_ref=src, dst_ref=table.at[origin * rows + r],
-            send_sem=line_send.at[direction, step, r], recv_sem=line_recv.at[direction, step, r],
-            device_id={"grp": g + 1 if direction == 0 else g - 1},
-        )
-
-    merge_sources = ((2, 3, 1, 0), (4, 5, 1, 0))
-
-    def grp_meta(k):
-        return pltpu.make_async_remote_copy(
-            src_ref=grp_out, dst_ref=grp_in.at[g], send_sem=gmeta_send.at[k], recv_sem=gmeta_recv.at[k],
-            device_id={"grp": lax.rem(g + k, n_grp)},
-        )
-
-    def dom_meta(k):
-        target = partner(k)
-        return pltpu.make_async_remote_copy(
-            src_ref=dom_out.at[target], dst_ref=dom_in.at[me], send_sem=dmeta_send.at[k], recv_sem=dmeta_recv.at[k],
-            device_id={"dom": target},
-        )
-
-    def halo_copy(k):
-        target = partner(k)
-        return pltpu.make_async_remote_copy(
-            src_ref=outgoing.at[pl.ds(target * hs, hs)], dst_ref=table.at[pl.ds(near_count + me * hs, hs)],
-            send_sem=halo_send.at[k], recv_sem=halo_recv.at[k],
-            device_id={"dom": target},
-        )
-
     for k in range(1, n_grp):
         grp_meta(k).start()
 
@@ -136,12 +145,8 @@
         return carry
 
     lax.fori_loop(1, n_dom, start_dom_meta, 0)
-    can_send = (g < n_grp - 1, g > 0)
-    for r in range(rows):
-        for direction in range(2):
-            @pl.when(can_send[direction])
-            def _():
-                line_copy(direction, 0, r, prolong_in.at[r], g).start()
+    for r in range(1, rows):
+        send_own(r)
 
     own_load.wait()
 
@@ -365,7 +370,7 @@
                 ap[at + 1] = jnp.where(low, turned, rest).astype(jnp.bfloat16)
             return carry
 
-        lax.fori_loop(0, plane_ids // 4, four, 0)
+        lax.fori_loop(0, plane_ids // 4, four, 0, unroll=4)
 
     def near_index(origin):
         return lambda r, e: plan_s[origin, r, e]
@@ -385,8 +390,8 @@
             device_id={"dom": partner(k)},
         )
 
-    def slot_rows(s, owner_dom, slot, at):
-        first, last = stages[s][1:]
+    def slot_rows(s, owner_dom, slot, at, window=None):
+        first, last = stages[s][1:] if window is None else window
         line = hs + owner[0, slot]
         for c in range(first, last, 2):
             right = jnp.concatenate([ap[plan_s[sort_at + owner_dom, line, c + h]] for h in range(2)], axis=1)
@@ -481,15 +486,21 @@
 
     def exchange_merged():
         s = len(stages) - 1
-        before = None
+        ready = []
         for k in (7, 6, 5, 3, 4, 2, 1):
-            slot_rows(s, partner(k), partner(k) * cap, k)
-            if before is not None:
-                for copy in feeds_of(before) + direct_of(before):
+            for way in range(2):
+                slot_rows(s, partner(k), partner(k) * cap, k, way_window(way))
+                for copy in ready:
                     copy.start()
-            before = k
+                if k > 5:
+                    ready = [feeds_of(k)[way]]
+                elif k == 1:
+                    ready = direct_of(k) if way == 1 else []
+                else:
+                    direct = (way == 0) == (k < 4)
+                    ready = direct_of(k) if direct else feeds_of(k)
         own_slots(s)
-        for copy in feeds_of(before) + direct_of(before):
+        for copy in ready:
             copy.start()
         for way in range(2):
             window = way_window(way)

time: 60.2 us -> 57.2 us (0.950)
  Pallas kernels: 58.4 us -> 55.6 us
    pallas_call x1, Pallas kernels: 58.4 us -> 55.6 us  [per_device(): result, late = call(by_distance, through_chip, 0, 'coarse_rows')(*args)]
where the time goes in v6:
time: 57.2 us; the launch traced here: 57 us
  Pallas kernels  55.6 us (97%)
  local copies, waits for them, and re-layouts  0.8 us (1%)
  between operations  0.63 us (1%)
    pallas_call x1, Pallas kernels, per_device(): result, late = call(by_distance, through_chip, 0, 'coarse_rows')(*args)  55.6 us

profile of v6, /device:TPU:0, one launch (start us, length us, event | category | flops | bytes accessed | tf_op | source)
XLA Modules:
  0.0 57.0 jit_solution(2600029087060598473)
XLA Ops:
  0.0 55.6 %coarse_rows.1 = (f32[2,16,4096]{2,1,0:T(8,128)S(1)}, s32[1,1]{1,0:T(1,128)}) custom-call(s32[4,16]{1,0:T(4,128)} %cols.1, s32[4]{0:T(128)} %halo.1, s32[4,8]{1,0:T(4,128)} %slots.1, s32[1,8]{1,0:T(1,128)} %picked.1, s32[1,16]{1,0:T(1,128)} %owner.1, s32[4,8]{1,0:T(4,128)} %prolong_cols.1, s32[2,16]{1,0:T(2,128)} %pattern.1, f32[4,8,4096]{2,1,0:T(8,128)} %prolong_in.1, ...), custom_call_target="tpu_custom_call" | custom-call | tf_op jit(solution)/shard_map/coarse_rows/pallas_call | solution.py:731
  56.2 0.8 %copy.15 = f32[2,16,4096]{2,1,0:T(8,128)} copy(f32[2,16,4096]{2,1,0:T(8,128)S(1)} %get-tuple-element.41) | data formatting | bytes 1048576
  (1 shorter events, 0.0 us)

commit v7 on v6

--- a/solution.py
+++ b/solution.py
@@ -633,7 +633,7 @@
                 )
         return carry
 
-    lax.fori_loop(0, owned, place_row, 0)
+    lax.fori_loop(0, owned, place_row, 0, unroll=True)
 
     def drain(k, carry):
         halo_copy(k).wait_send()

time: 57.2 us -> 57.1 us (level)
  no operation moved by 1% of the time
where the time goes in v7:
time: 57.1 us; the launch traced here: 57 us
  Pallas kernels  55.5 us (97%)
  local copies, waits for them, and re-layouts  0.8 us (1%)
  between operations  0.63 us (1%)
    pallas_call x1, Pallas kernels, per_device(): result, late = call(by_distance, through_chip, 0, 'coarse_rows')(*args)  55.5 us

profile of v7, /device:TPU:0, one launch (start us, length us, event | category | flops | bytes accessed | tf_op | source)
XLA Modules:
  0.0 57.0 jit_solution(16256819887472621541)
XLA Ops:
  0.0 55.5 %coarse_rows.1 = (f32[2,16,4096]{2,1,0:T(8,128)S(1)}, s32[1,1]{1,0:T(1,128)}) custom-call(s32[4,16]{1,0:T(4,128)} %cols.1, s32[4]{0:T(128)} %halo.1, s32[4,8]{1,0:T(4,128)} %slots.1, s32[1,8]{1,0:T(1,128)} %picked.1, s32[1,16]{1,0:T(1,128)} %owner.1, s32[4,8]{1,0:T(4,128)} %prolong_cols.1, s32[2,16]{1,0:T(2,128)} %pattern.1, f32[4,8,4096]{2,1,0:T(8,128)} %prolong_in.1, ...), custom_call_target="tpu_custom_call" | custom-call | tf_op jit(solution)/shard_map/coarse_rows/pallas_call | solution.py:731
  56.2 0.8 %copy.15 = f32[2,16,4096]{2,1,0:T(8,128)} copy(f32[2,16,4096]{2,1,0:T(8,128)S(1)} %get-tuple-element.41) | data formatting | bytes 1048576
  (1 shorter events, 0.0 us)
